TPU v7x, 256 devices: a whole 4x4x8 slice. The times are simulated.
256 devices in a mesh: row: 8 (over z_hi, x), col: 32 (over y, z_lo, core).
Axes of the slice: x: 4, y: 4, z: 8 (z_hi: 2, z_lo: 4; z = z_hi * 4 + z_lo), core: 2. Of those that a mesh axis runs over, the one named last changes fastest.
Arguments:
- inv_anc: float32 [8, 32, 48, 12288], P(None, 'col', None, 'row'), may hold values from -6 to 6
- factor_cols: float32 [4, 12288, 256], P(None, ('row', 'col')), may hold values from -0.0546875 to 0.0546875
- couple: float32 [6, 256, 256], replicated, may hold values from -0.1875 to 0.1875
- diag_inv: float32 [4, 256, 256], replicated, may hold values from -6 to 6, as said below
- pattern: int32 [4, 48], replicated, may hold values 0 or 1
- parent: int32 [4], replicated, may hold values from 0 to 4, as said below
Outputs:
- inv_cols: float32 [4, 12288, 256], P(None, ('row', 'col'))
- win_cols: float32 [6, 256, 256], replicated
- win_diag: float32 [4, 256, 256], replicated
Inputs may be any that keep to these rules, and one draw needn't show every extreme that they name: parent[0] is 4, meaning a parent in the ancestor set; for j of 1 or more parent[j] is an earlier supernode or 4. Each diag_inv[j] is symmetric.
All inputs are finite; a program needn't handle non-finite values.
Results may differ from a plain program's by a relative error of at most 0.0001.
Values sent between devices are 32-bit elements; how exact they have to be, the bound alone decides.
No kernel may reach another device: no remote copies, remote signals or barrier semaphores. Data moves between devices by JAX's collectives and lax.ppermute only.
A program may use at most 64 MiB of HBM per device.

v0:
```python
import jax
import jax.numpy as jnp
from jax import lax
from jax.sharding import PartitionSpec as P

W = 256
NSUP = 4
exact_mode = lax.Precision.HIGHEST


def product(left, right):
    return jnp.dot(left, right, precision=exact_mode, preferred_element_type=jnp.float32)


def ancestry(parent):
    linked = {}
    for j in range(NSUP):
        for m in range(j):
            linked_now = parent[j] == m
            for p in range(m + 1, j):
                linked_now = linked_now | (parent[j] == p) & linked[p, m]
            linked[j, m] = linked_now
    return linked


def couplings(couple, parent):
    linked = ancestry(parent)
    blocks = {}
    for j in range(NSUP):
        for m in range(j):
            blocks[j, m] = couple[j * (j - 1) // 2 + m] * linked[j, m].astype(jnp.float32)
    return blocks


def window_blocks(crossed, diag_terms, diag_inv, blocks):
    off_diag = {}
    diagonal = []

    def lookup_block(first, second):
        if first == second:
            return diagonal[first]
        if first < second:
            return off_diag[second, first]
        return off_diag[first, second].T

    for j in range(NSUP):
        for m in range(j):
            running = crossed[j, m]
            for q in range(j):
                running = running + product(lookup_block(m, q), blocks[j, q])
            off_diag[j, m] = -running
        diag_value = diag_inv[j] - diag_terms[j]
        for m in range(j):
            diag_value = diag_value - product(blocks[j, m].T, off_diag[j, m])
        diagonal.append(diag_value)
    pair_list = [off_diag[j, m] for j in range(NSUP) for m in range(j)]
    return (jnp.stack(pair_list), jnp.stack(diagonal))


def shards(inv_anc, factor_cols, couple, diag_inv, pattern, parent):
    col_count = lax.axis_size("col")
    local_block = inv_anc.reshape(inv_anc.shape[0] * inv_anc.shape[2], inv_anc.shape[3])
    rows_here = factor_cols.shape[1]
    first_row = (lax.axis_index("row") * col_count + lax.axis_index("col")) * rows_here
    row_ids = first_row + jnp.arange(rows_here, dtype=jnp.int32)
    block_ids = row_ids // W
    one_hot = (block_ids[:, None] == jnp.arange(pattern.shape[1], dtype=jnp.int32)[None, :]).astype(
        jnp.float32
    )
    row_mask = product(one_hot, pattern.astype(jnp.float32).T)
    masked = factor_cols * row_mask.T[:, :, None]
    blocks = couplings(couple, parent)
    columns = []
    for j in range(NSUP):
        partial_value = product(local_block, lax.all_gather(masked[j], "col", axis=0, tiled=True))
        summed = lax.psum_scatter(partial_value, "row", scatter_dimension=0, tiled=True)
        for m in range(j):
            summed = summed + product(columns[m], blocks[j, m])
        columns.append(-summed)
    crossed = {}
    diag_terms = []
    for j in range(NSUP):
        products = [product(columns[m].T, masked[j]) for m in range(j)]
        products.append(product(masked[j].T, columns[j]))
        summed_terms = lax.psum(jnp.stack(products), ("row", "col"))
        for m in range(j):
            crossed[j, m] = summed_terms[m]
        diag_terms.append(summed_terms[j])
    pair_blocks, diagonal = window_blocks(crossed, diag_terms, diag_inv, blocks)
    return (jnp.stack(columns), pair_blocks, diagonal)


def solution(mesh):
    in_specs = (P(None, "col", None, "row"), P(None, ("row", "col"), None), P(), P(), P(), P())
    out_specs = (P(None, ("row", "col"), None), P(), P())
    return jax.shard_map(shards, mesh=mesh, in_specs=in_specs, out_specs=out_specs, check_vma=False)
```

profile of v0, /device:TPU:97, one launch (start us, length us, event | category | flops | bytes accessed | tf_op | source)
XLA Modules:
  0.0 888.4 jit_solution(3892370437769683290)
XLA Ops:
  7.2 1.0 convolution_bitcast_fusion.10
  8.3 1.0 broadcast_multiply_fusion
  9.3 0.7 fusion.117
  10.1 0.7 all-gather.11.cloned.1.call-update
  10.8 0.7 all-gather.13.cloned.1.call-update
  11.5 0.5 all-gather.15.cloned.1.call-update
  12.1 58.4 %all-gather.9.cloned.1.call-done = f32[1,1536,256]{2,1,0:T(8,128)} async-done(((f32[1,48,256]{2,1,0:T(8,128)}), f32[1,1536,256]{2,1,0:T(8,128)}) %all-gather.9.cloned.1.call-update) | async-done | bytes 1572880 | tf_op jit(solution)/shard_map/all_gather | solution.py:75
  70.5 6.5 fusion.8
  77.0 0.9 copy.20
  78.0 52.5 %all-gather.11.cloned.1.call-done = f32[1,1536,256]{2,1,0:T(8,128)} async-done(((f32[1,48,256]{2,1,0:T(8,128)}), f32[1,1536,256]{2,1,0:T(8,128)}) %all-gather.11.cloned.1.call-update) | async-done | bytes 1572880 | tf_op jit(solution)/shard_map/all_gather | solution.py:75
  130.5 6.5 fusion.11
  137.0 0.9 copy.22
  138.2 52.8 %all-gather.13.cloned.1.call-done = f32[1,1536,256]{2,1,0:T(8,128)} async-done(((f32[1,48,256]{2,1,0:T(8,128)}), f32[1,1536,256]{2,1,0:T(8,128)}) %all-gather.13.cloned.1.call-update) | async-done | bytes 1572880 | tf_op jit(solution)/shard_map/all_gather | solution.py:75
  191.1 6.5 fusion.14
  197.5 0.9 copy.24
  198.5 0.6 fusion.118
  202.9 48.6 %all-gather.15.cloned.1.call-done = f32[1,1536,256]{2,1,0:T(8,128)} async-done(((f32[1,48,256]{2,1,0:T(8,128)}), f32[1,1536,256]{2,1,0:T(8,128)}) %all-gather.15.cloned.1.call-update) | async-done | bytes 1572880 | tf_op jit(solution)/shard_map/all_gather | solution.py:75
  251.5 6.5 fusion.17
  258.0 0.9 copy.26
  258.9 0.5 all-reduce.3.cloned.1.call-start
  259.4 76.6 %reduce-scatter.13.cloned.1.call-done = f32[48,256]{1,0:T(8,128)} async-done(((f32[384,256]{1,0:T(8,128)}), f32[48,256]{1,0:T(8,128)}) %reduce-scatter.13.cloned.1.call-update) | async-done | bytes 49168
  336.0 0.9 copy.21
  336.9 84.0 %reduce-scatter.15.cloned.1.call-done = f32[48,256]{1,0:T(8,128)} async-done(((f32[384,256]{1,0:T(8,128)}), f32[48,256]{1,0:T(8,128)}) %reduce-scatter.15.cloned.1.call-update) | async-done | bytes 49168 | tf_op jit(solution)/shard_map/reduce_scatter | solution.py:76
  420.9 1.3 fusion.29
  422.2 83.7 %reduce-scatter.17.cloned.1.call-done = f32[48,256]{1,0:T(8,128)} async-done(((f32[384,256]{1,0:T(8,128)}), f32[48,256]{1,0:T(8,128)}) %reduce-scatter.17.cloned.1.call-update) | async-done | bytes 49168 | tf_op jit(solution)/shard_map/reduce_scatter | solution.py:76
  505.9 1.3 convolution_add_fusion.18
  507.2 1.2 fusion.28
  508.5 1.1 convolution_bitcast_fusion.5
  509.6 1.1 convolution_bitcast_fusion.7
  510.7 1.1 convolution_bitcast_fusion.6
  511.8 1.1 convolution_bitcast_fusion.8
  513.0 1.1 convolution_bitcast_fusion.9
  514.4 1.1 convolution_bitcast_fusion.2
  515.9 1.1 convolution_bitcast_fusion
  517.0 74.6 %reduce-scatter.19.cloned.1.call-done = f32[48,256]{1,0:T(8,128)} async-done(((f32[384,256]{1,0:T(8,128)}), f32[48,256]{1,0:T(8,128)}) %reduce-scatter.19.cloned.1.call-update) | async-done | bytes 49168 | tf_op jit(solution)/shard_map/reduce_scatter | solution.py:76
  591.5 1.4 convolution_add_fusion.17
  592.9 1.2 convolution_add_fusion.15
  594.1 1.2 fusion.27
  595.4 0.4 convolution_bitcast_fusion.4
  595.8 0.8 pad_maximum_fusion.3
  596.7 0.9 pad_maximum_fusion.2
  597.6 1.0 pad_maximum_fusion
  598.8 0.7 pad_maximum_fusion.4
  599.4 267.4 %all-reduce.3.cloned.1.call-done = (f32[2,256,256]{2,1,0:T(8,128)}, f32[1,256,256]{2,1,0:T(8,128)}, f32[3,256,256]{2,1,0:T(8,128)}, f32[4,256,256]{2,1,0:T(8,128)}) async-done(((f32[2,256,256]{2,1,0:T(8,128)}, f32[1,256,256]{2,1,0:T(8,128)}, f32[3,256,256]{2,1,0:T(8,128)}, f32[4,256,256]{2,1,0:T(8,128)}), (f32[2,256,256]{2,1,0:T(8,128)}, f32[1,256,256]{2,1,0:T(8,128)}, f32[3,256,256]{2,1,0:T(8,128)}, ...) | async-done | bytes 2621456 | tf_op jit(solution)/shard_map/psum | solution.py:85
  866.8 1.2 slice_subtract_fusion.3
  868.1 1.5 convolution_add_fusion.12
  869.6 1.3 convolution_add_fusion.8
  870.9 0.4 bitcast_dynamic-update-slice_fusion.5
  871.4 0.6 convolution_subtract_fusion.5
  872.0 0.4 bitcast_dynamic-update-slice_fusion.4
  872.6 0.6 convolution_add_fusion.2
  873.2 0.6 convolution_subtract_fusion.4
  873.8 0.6 convolution_add_fusion.10
  874.4 0.6 convolution_add_fusion.5
  875.8 0.4 bitcast_dynamic-update-slice_fusion.3
  876.2 0.4 bitcast_dynamic-update-slice_fusion.2
  876.6 0.6 convolution_subtract_fusion.2
  877.2 0.6 convolution_subtract_fusion.3
  877.8 0.8 convolution_add_fusion.1
  878.6 0.4 bitcast_dynamic-update-slice_fusion.1
  879.0 0.6 convolution_subtract_fusion.1
  879.6 0.4 bitcast_dynamic-update-slice_fusion
  880.0 0.6 fusion.20
  880.6 1.0 pad_maximum_fusion.1
  (49 shorter events, 2.5 us)
Async XLA Ops:
  7.2 63.3 %copy-start = (f32[8,1,48,1536]{3,2,1,0:T(8,128)S(1)}, f32[8,1,48,1536]{3,2,1,0:T(8,128)}, u32[]{:S(2)}) copy-start(f32[8,1,48,1536]{3,2,1,0:T(8,128)} %param.6) | copy-start | bytes 7077892
  7.2 63.3 %all-gather.9.cloned.1.call-start = ((), (), s32[]{:S(2)}) async-start(), calls=%async_computation.4 | async-start | bytes 1622016 | tf_op jit(solution)/shard_map/all_gather | solution.py:75
  10.0 120.5 %all-gather.11.cloned.1.call-start = ((), (), s32[]{:S(2)}) async-start(), calls=%async_computation.5 | async-start | bytes 1622016 | tf_op jit(solution)/shard_map/all_gather | solution.py:75
  10.8 180.3 %all-gather.13.cloned.1.call-start = ((), (), s32[]{:S(2)}) async-start(), calls=%async_computation.6 | async-start | bytes 1622016 | tf_op jit(solution)/shard_map/all_gather | solution.py:75
  11.5 240.0 %all-gather.15.cloned.1.call-start = ((), (), s32[]{:S(2)}) async-start(), calls=%async_computation.7 | async-start | bytes 1622016 | tf_op jit(solution)/shard_map/all_gather | solution.py:75
  12.1 324.0 %reduce-scatter.13.cloned.1.call-start = ((), (), s32[]{:S(2)}) async-start(), calls=%async_computation.8 | async-start | bytes 442368
  77.9 343.0 %reduce-scatter.15.cloned.1.call-start = ((), (), s32[]{:S(2)}) async-start(), calls=%async_computation.9 | async-start | bytes 442368 | tf_op jit(solution)/shard_map/reduce_scatter | solution.py:76
  137.9 60.6 %copy-start.13 = (s32[4]{0:T(128)S(1)}, s32[4]{0:T(128)}, u32[]{:S(2)}) copy-start(s32[4]{0:T(128)} %param.11) | copy-start | bytes 52
  137.9 368.0 %reduce-scatter.17.cloned.1.call-start = ((), (), s32[]{:S(2)}) async-start(), calls=%async_computation.10 | async-start | bytes 442368 | tf_op jit(solution)/shard_map/reduce_scatter | solution.py:76
  198.5 393.1 %reduce-scatter.19.cloned.1.call-start = ((), (), s32[]{:S(2)}) async-start(), calls=%async_computation.11 | async-start | bytes 442368 | tf_op jit(solution)/shard_map/reduce_scatter | solution.py:76
  258.9 607.9 %all-reduce.3.cloned.1.call-start = ((), (), s32[]{:S(2)}) async-start(), calls=%async_computation.12 | async-start | bytes 5242880 | tf_op jit(solution)/shard_map/psum | solution.py:85
  591.5 4.3 copy-start.6
  591.5 5.1 copy-start.4
  591.5 5.1 copy-start.5
  595.4 2.2 copy-start.7
  595.4 2.2 copy-start.8
  595.4 2.2 copy-start.9
  866.8 2.7 copy-start.1
  866.8 4.1 copy-start.11
  868.0 3.3 copy-start.2
  871.3 1.2 copy-start.3
  871.3 1.8 copy-start.10
  880.0 1.7 copy-start.12
Sparse Core Ops, SparseCore 0:
  10.4 60.0 all-gather.8
  72.4 58.0 all-gather.10
  132.9 58.0 all-gather.12
  193.3 58.0 all-gather.14
  255.8 80.2 reduce-scatter.12
  339.8 81.0 reduce-scatter.14
  424.8 81.1 reduce-scatter.16
  510.4 81.1 reduce-scatter.18
  598.8 267.9 all-reduce.2
where the time goes:
time: 897 us; the launch traced here: 888 us
  waiting for transfers between devices  800 us (89%)
  matrix products  55.6 us (6%)
  between operations  18.2 us (2%)
    psum x1, waiting for transfers between devices, shards(): summed_terms = lax.psum(jnp.stack(products), ('row', 'col'))  267 us
    reduce_scatter x3, waiting for transfers between devices, shards(): lax.psum_scatter(partial_value, 'row', scatter_dimension=0, tiled=True)  242 us
    all_gather x4, waiting for transfers between devices, shards(): lax.all_gather(masked[j], 'col', axis=0, tiled=True)  212 us
    unnamed x10, waiting for transfers between devices  78.6 us
    dot_general x41, matrix products, product(): jnp.dot(left, right, precision=exact_mode, preferred_element_type=jnp.flo...  55.6 us
  transfers between devices with their start and end apart: 9, of which 9 were waited for; matrix products, arithmetic and copies ran while one was open for 5% of the time, Pallas kernels for 0%

commit v1 on v0

--- a/solution.py
+++ b/solution.py
@@ -6,6 +6,13 @@
 W = 256
 NSUP = 4
 exact_mode = lax.Precision.HIGHEST
+
+
+def swapped_in(array, axis, d):
+    size = lax.axis_size(axis)
+    tiles = jnp.stack([array for _ in range(size)])
+    tiles = lax.all_to_all(tiles, axis, split_axis=0, concat_axis=0)
+    return jnp.concatenate(tiles, axis=d)
 
 
 def product(left, right):
@@ -72,7 +79,7 @@
     blocks = couplings(couple, parent)
     columns = []
     for j in range(NSUP):
-        partial_value = product(local_block, lax.all_gather(masked[j], "col", axis=0, tiled=True))
+        partial_value = product(local_block, swapped_in(masked[j], "col", 0))
         summed = lax.psum_scatter(partial_value, "row", scatter_dimension=0, tiled=True)
         for m in range(j):
             summed = summed + product(columns[m], blocks[j, m])

time: 897 us -> 796 us (0.89)
  waiting for transfers between devices: 800 us -> 554 us
  blocking collectives: 0 us -> 131 us
  starting transfers between devices: 1.08 us -> 15.7 us
    all_gather x4 -> x0, waiting for transfers between devices: 212 us -> none  [shards(): lax.all_gather(masked[j], 'col', axis=0, tiled=True)]
    all_to_all x0 -> x3, blocking collectives: none -> 131 us  [swapped_in(): tiles = lax.all_to_all(tiles, axis, split_axis=0, concat_axis=0)]
    unnamed x10 -> x6, waiting for transfers between devices: 78.6 us -> 33.8 us
    all_to_all x0 -> x1, waiting for transfers between devices: none -> 10.8 us  [swapped_in(): tiles = lax.all_to_all(tiles, axis, split_axis=0, concat_axis=0)]
  transfers between devices with their start and end apart: 9 -> 6, of which waited for: 9 -> 6; matrix products, arithmetic and copies ran while one was open for 5% -> 6% of each run, Pallas kernels for 0% -> 0%
where the time goes in v1:
time: 796 us; the launch traced here: 789 us
  waiting for transfers between devices  554 us (70%)
  blocking collectives  131 us (16%)
  matrix products  55.6 us (7%)
  between operations  18.3 us (2%)
  starting transfers between devices  15.7 us (2%)
    psum x1, waiting for transfers between devices, shards(): summed_terms = lax.psum(jnp.stack(products), ('row', 'col'))  268 us
    reduce_scatter x3, waiting for transfers between devices, shards(): lax.psum_scatter(partial_value, 'row', scatter_dimension=0, tiled=True)  242 us
    all_to_all x3, blocking collectives, swapped_in(): tiles = lax.all_to_all(tiles, axis, split_axis=0, concat_axis=0)  131 us
    dot_general x41, matrix products, product(): jnp.dot(left, right, precision=exact_mode, preferred_element_type=jnp.flo...  55.6 us
    unnamed x6, waiting for transfers between devices  33.8 us
  transfers between devices with their start and end apart: 6, of which 6 were waited for; matrix products, arithmetic and copies ran while one was open for 6% of the time, Pallas kernels for 0%

profile of v1, /device:TPU:97, one launch (start us, length us, event | category | flops | bytes accessed | tf_op | source)
XLA Modules:
  0.0 789.3 jit_solution(14796008503216314915)
XLA Ops:
  7.2 1.0 convolution_bitcast_fusion.14
  8.2 1.0 broadcast_multiply_fusion
  9.5 45.3 %all_to_all.20 = f32[32,48,256]{2,1,0:T(8,128)} all-to-all(f32[32,48,256]{2,1,0:T(8,128)S(1)} %stack.104), channel_id=1, replica_groups=mesh['row'=8,'col'=32] {'col'}, dimensions={0} | all-to-all | bytes 3145728 | tf_op jit(solution)/shard_map/all_to_all | solution.py:14
  54.9 42.9 %all_to_all.21 = f32[32,48,256]{2,1,0:T(8,128)} all-to-all(f32[32,48,256]{2,1,0:T(8,128)S(1)} %stack.102), channel_id=1, replica_groups=mesh['row'=8,'col'=32] {'col'}, dimensions={0} | all-to-all | bytes 3145728 | tf_op jit(solution)/shard_map/all_to_all | solution.py:14
  98.0 42.9 %all_to_all.22 = f32[32,48,256]{2,1,0:T(8,128)} all-to-all(f32[32,48,256]{2,1,0:T(8,128)S(1)} %stack.100), channel_id=1, replica_groups=mesh['row'=8,'col'=32] {'col'}, dimensions={0} | all-to-all | bytes 3145728 | tf_op jit(solution)/shard_map/all_to_all | solution.py:14
  140.9 1.3 stack.106
  142.2 6.5 all-to-all-start.3
  148.7 6.5 convolution_bitcast_fusion.3
  155.2 0.9 copy.20
  156.1 0.4 reduce-scatter.15.cloned.1.call-start
  156.6 6.5 convolution_bitcast_fusion.2
  163.0 0.9 copy.22
  164.0 6.5 convolution_bitcast_fusion.1
  170.5 0.9 copy.24
  171.5 0.6 fusion.77
  176.0 10.8 %all-to-all-done.3 = f32[32,48,256]{2,1,0:T(8,128)} async-done(((f32[32,48,256]{2,1,0:T(8,128)}), f32[32,48,256]{2,1,0:T(8,128)}, u32[]{:S(2)}, u32[]{:S(2)}) %all-to-all-start.3) | async-done | bytes 1572896 | tf_op jit(solution)/shard_map/all_to_all | solution.py:14
  186.9 6.5 convolution_bitcast_fusion
  193.4 0.9 copy.26
  194.3 8.7 %all-reduce.3.cloned.1.call-start = ((), (), s32[]{:S(2)}) async-start(), calls=%async_computation.12 | async-start | bytes 5242880 | tf_op jit(solution)/shard_map/psum | solution.py:92
  203.0 33.7 %reduce-scatter.13.cloned.1.call-done = f32[48,256]{1,0:T(8,128)} async-done(((f32[384,256]{1,0:T(8,128)}), f32[48,256]{1,0:T(8,128)}) %reduce-scatter.13.cloned.1.call-update) | async-done | bytes 49168
  236.7 0.9 copy.21
  237.6 84.1 %reduce-scatter.15.cloned.1.call-done = f32[48,256]{1,0:T(8,128)} async-done(((f32[384,256]{1,0:T(8,128)}), f32[48,256]{1,0:T(8,128)}) %reduce-scatter.15.cloned.1.call-update) | async-done | bytes 49168 | tf_op jit(solution)/shard_map/reduce_scatter | solution.py:83
  321.8 1.3 fusion.9
  323.1 83.7 %reduce-scatter.17.cloned.1.call-done = f32[48,256]{1,0:T(8,128)} async-done(((f32[384,256]{1,0:T(8,128)}), f32[48,256]{1,0:T(8,128)}) %reduce-scatter.17.cloned.1.call-update) | async-done | bytes 49168 | tf_op jit(solution)/shard_map/reduce_scatter | solution.py:83
  406.8 1.3 convolution_add_fusion.18
  408.1 1.2 fusion.8
  409.3 1.1 convolution_bitcast_fusion.9
  410.4 1.1 convolution_bitcast_fusion.11
  411.5 1.1 convolution_bitcast_fusion.10
  412.7 1.1 convolution_bitcast_fusion.12
  413.8 1.1 convolution_bitcast_fusion.13
  415.3 1.1 convolution_bitcast_fusion.6
  416.7 1.1 convolution_bitcast_fusion.4
  417.8 74.4 %reduce-scatter.19.cloned.1.call-done = f32[48,256]{1,0:T(8,128)} async-done(((f32[384,256]{1,0:T(8,128)}), f32[48,256]{1,0:T(8,128)}) %reduce-scatter.19.cloned.1.call-update) | async-done | bytes 49168 | tf_op jit(solution)/shard_map/reduce_scatter | solution.py:83
  492.2 1.4 convolution_add_fusion.17
  493.6 1.2 convolution_add_fusion.15
  494.8 1.2 fusion.7
  496.1 0.4 convolution_bitcast_fusion.8
  496.5 0.8 pad_maximum_fusion.3
  497.3 0.9 pad_maximum_fusion.2
  498.3 1.0 pad_maximum_fusion
  499.4 0.7 pad_maximum_fusion.4
  500.1 267.5 %all-reduce.3.cloned.1.call-done = (f32[2,256,256]{2,1,0:T(8,128)}, f32[1,256,256]{2,1,0:T(8,128)}, f32[3,256,256]{2,1,0:T(8,128)}, f32[4,256,256]{2,1,0:T(8,128)}) async-done(((f32[2,256,256]{2,1,0:T(8,128)}, f32[1,256,256]{2,1,0:T(8,128)}, f32[3,256,256]{2,1,0:T(8,128)}, f32[4,256,256]{2,1,0:T(8,128)}), (f32[2,256,256]{2,1,0:T(8,128)}, f32[1,256,256]{2,1,0:T(8,128)}, f32[3,256,256]{2,1,0:T(8,128)}, ...) | async-done | bytes 2621456 | tf_op jit(solution)/shard_map/psum | solution.py:92
  767.7 1.2 slice_subtract_fusion.3
  768.9 1.5 convolution_add_fusion.12
  770.4 1.3 convolution_add_fusion.8
  771.8 0.4 bitcast_dynamic-update-slice_fusion.5
  772.2 0.6 convolution_subtract_fusion.5
  772.8 0.4 bitcast_dynamic-update-slice_fusion.4
  773.4 0.6 convolution_add_fusion.2
  774.0 0.6 convolution_subtract_fusion.4
  774.6 0.6 convolution_add_fusion.10
  775.2 0.6 convolution_add_fusion.5
  776.2 0.4 convolution_add_fusion.4
  776.6 0.4 bitcast_dynamic-update-slice_fusion.3
  777.0 0.4 bitcast_dynamic-update-slice_fusion.2
  777.4 0.6 convolution_subtract_fusion.2
  778.0 0.6 convolution_subtract_fusion.3
  778.6 0.8 convolution_add_fusion.1
  779.4 0.4 bitcast_dynamic-update-slice_fusion.1
  779.8 0.6 convolution_subtract_fusion.1
  780.4 0.4 bitcast_dynamic-update-slice_fusion
  780.8 0.6 fusion
  781.5 1.0 pad_maximum_fusion.1
  (46 shorter events, 2.2 us)
Async XLA Ops:
  7.2 141.5 %copy-start = (f32[8,1,48,1536]{3,2,1,0:T(8,128)S(1)}, f32[8,1,48,1536]{3,2,1,0:T(8,128)}, u32[]{:S(2)}) copy-start(f32[8,1,48,1536]{3,2,1,0:T(8,128)} %param.6) | copy-start | bytes 7077892
  142.2 44.7 %all-to-all-start.3 = ((f32[32,48,256]{2,1,0:T(8,128)}), f32[32,48,256]{2,1,0:T(8,128)}, u32[]{:S(2)}, u32[]{:S(2)}) async-start(f32[32,48,256]{2,1,0:T(8,128)} %stack.106), calls=%async_computation.3 | async-start | bytes 3145728 | tf_op jit(solution)/shard_map/all_to_all | solution.py:14
  148.6 88.1 %reduce-scatter.13.cloned.1.call-start = ((), (), s32[]{:S(2)}) async-start(), calls=%async_computation.8 | async-start | bytes 442368
  156.1 165.6 %reduce-scatter.15.cloned.1.call-start = ((), (), s32[]{:S(2)}) async-start(), calls=%async_computation.9 | async-start | bytes 442368 | tf_op jit(solution)/shard_map/reduce_scatter | solution.py:83
  164.0 242.8 %reduce-scatter.17.cloned.1.call-start = ((), (), s32[]{:S(2)}) async-start(), calls=%async_computation.10 | async-start | bytes 442368 | tf_op jit(solution)/shard_map/reduce_scatter | solution.py:83
  164.0 7.5 copy-start.13
  171.5 320.7 %reduce-scatter.19.cloned.1.call-start = ((), (), s32[]{:S(2)}) async-start(), calls=%async_computation.11 | async-start | bytes 442368 | tf_op jit(solution)/shard_map/reduce_scatter | solution.py:83
  194.3 573.4 %all-reduce.3.cloned.1.call-start = ((), (), s32[]{:S(2)}) async-start(), calls=%async_computation.12 | async-start | bytes 5242880 | tf_op jit(solution)/shard_map/psum | solution.py:92
  492.2 4.3 copy-start.6
  492.2 5.1 copy-start.4
  492.2 5.1 copy-start.5
  496.0 2.2 copy-start.7
  496.0 2.2 copy-start.8
  496.1 2.2 copy-start.9
  767.7 2.7 copy-start.1
  767.7 4.1 copy-start.11
  768.9 3.3 copy-start.2
  772.2 1.2 copy-start.3
  772.2 1.8 copy-start.10
  780.8 1.7 copy-start.12
Sparse Core Ops, SparseCore 0:
  156.2 80.4 reduce-scatter.12
  240.6 81.1 reduce-scatter.14
  325.6 81.0 reduce-scatter.16
  411.1 81.0 reduce-scatter.18
  499.5 268.1 all-reduce.2
